TPU v7x, 256 devices: a whole 4x4x8 slice. The times are simulated.
256 devices in a mesh: row: 32 (over y, x, core), col: 8 (over z).
Axes of the slice: x: 4, y: 4, z: 8, core: 2. Of those that a mesh axis runs over, the one named last changes fastest.
Arguments:
- features: bfloat16 [32768, 512], P(('row', 'col')), may hold values from -6 to 6
- tile_data: bfloat16 [256, 32, 2, 128, 128], P('row', 'col'), as said below
- tile_ids: int32 [256, 32, 2], P('row', 'col'), may hold values from 0 to 7, as said below
- tile_counts: int32 [256, 32], P('row', 'col'), may hold values from 0 to 2, as said below
- hist_tiles: bfloat16 [256, 8, 128, 128], P('row', 'col'), may hold values from -0.1875 to 0.1875
- hist_ids: int32 [256, 8], P('row', 'col'), may hold values from 0 to 31
- hist_cache: bfloat16 [4096, 512], P('col'), may hold values from -6 to 6
- first_weight: bfloat16 [512, 512], replicated, may hold values from -0.25 to 0.25
- second_weight: bfloat16 [512, 512], replicated, may hold values from -0.25 to 0.25
- grad_out: bfloat16 [32768, 512], P(('row', 'col')), may hold values from -6 to 6
Outputs:
- embedding: bfloat16 [32768, 512], P(('row', 'col'))
- grad_first: float32 [512, 512], replicated
- grad_second: float32 [512, 512], replicated
Inputs may be any that keep to these rules, and one draw needn't show every extreme that they name: tile_ids[p, j, t] is a tile column within panel j; slots t >= tile_counts[p, j] are padding and must be ignored; the used slots of a tile row and panel name distinct columns; the matrix that the tiles describe is symmetric. `tile_counts`: the count depends only on the block row of the tile row and on the panel. `tile_data`: padded slots hold arbitrary values.
All inputs are finite; a program needn't handle non-finite values.
Results may differ from a plain program's by a relative error of at most 0.018.
Values may be sent and summed in bfloat16 or wider, within the bound.
No kernel may reach another device: no remote copies, remote signals or barrier semaphores. Data moves between devices by JAX's collectives and lax.ppermute only.
A program may use at most 128 MiB of HBM per device.

v0:
```python
import math
import jax
import jax.numpy as jnp
from jax import lax
from jax.sharding import PartitionSpec as P


def spread(shard, axis, root):
    mine = lax.axis_index(axis) == root
    return lax.psum(jnp.where(mine, shard, jnp.zeros_like(shard)), axis)


def pick_tiles(panel_rows, tile_data, tile_ids, tile_counts):
    tile_rows = tile_ids.shape[0]
    slot_count = tile_ids.shape[1]
    tile_size = tile_data.shape[-1]
    blocks = panel_rows.reshape(tile_rows, tile_size, panel_rows.shape[1])
    picked = blocks[tile_ids]
    keep_mask = (jnp.arange(slot_count)[None, :] < tile_counts[:, None]).astype(tile_data.dtype)
    masked = tile_data * keep_mask[:, :, None, None]
    product = jnp.einsum("atij,atjf->aif", masked, picked, preferred_element_type=jnp.float32)
    return product.reshape(tile_rows * tile_size, panel_rows.shape[1])


def aggregate(source, tile_data, tile_ids, tile_counts):
    section_total = tile_data.shape[1]
    col_index = lax.axis_index("col")
    running = jnp.zeros(source.shape, jnp.float32)
    for section_num in range(section_total):
        panel_rows = spread(source, "row", col_index * section_total + section_num)
        running = running + pick_tiles(
            panel_rows,
            tile_data[:, section_num],
            tile_ids[:, section_num],
            tile_counts[:, section_num],
        )
    return running


def local(
    features,
    tile_data,
    tile_ids,
    tile_counts,
    hist_tiles,
    hist_ids,
    hist_cache,
    first_weight,
    second_weight,
    grad_out,
):
    share_rows = features.shape[0]
    node_count = share_rows * lax.axis_size("row") * lax.axis_size("col")
    norm_scale = 1.0 / math.sqrt(node_count)
    contract_rows = (((0,), (0,)), ((), ()))
    feat_panel = lax.all_gather(features, "col", axis=0, tiled=True)
    first_sum = aggregate(feat_panel, tile_data, tile_ids, tile_counts)
    first_agg = lax.psum_scatter(
        first_sum.astype(jnp.bfloat16), "col", scatter_dimension=0, tiled=True
    )
    first_pre = jnp.dot(first_agg, first_weight, preferred_element_type=jnp.float32)
    hidden_share = jax.nn.silu(first_pre).astype(jnp.bfloat16)
    hidden_panel = lax.all_gather(hidden_share, "col", axis=0, tiled=True)
    second_sum = aggregate(hidden_panel, tile_data, tile_ids, tile_counts)
    tile_size = hist_tiles.shape[-1]
    feat_width = hist_cache.shape[1]
    whole_cache = lax.all_gather(hist_cache, "col", axis=0, tiled=True)
    cache_blocks = whole_cache.reshape(-1, tile_size, feat_width)
    picked = cache_blocks[hist_ids]
    history = jnp.einsum("ahij,ahjf->aif", hist_tiles, picked, preferred_element_type=jnp.float32)
    second_sum = second_sum + history.reshape(second_sum.shape)
    second_agg = lax.psum_scatter(
        second_sum.astype(jnp.bfloat16), "col", scatter_dimension=0, tiled=True
    )
    embedding = jnp.dot(second_agg, second_weight, preferred_element_type=jnp.float32).astype(
        jnp.bfloat16
    )
    grad_agg = lax.dot_general(
        grad_out, second_weight, (((1,), (1,)), ((), ())), preferred_element_type=jnp.float32
    ).astype(jnp.bfloat16)
    second_term = (
        lax.dot_general(second_agg, grad_out, contract_rows, preferred_element_type=jnp.float32)
        * norm_scale
    )
    grad_second = lax.psum(second_term, ("row", "col"))
    grad_panel = lax.all_gather(grad_agg, "col", axis=0, tiled=True)
    back_sum = aggregate(grad_panel, tile_data, tile_ids, tile_counts)
    grad_hidden = lax.psum_scatter(
        back_sum.astype(jnp.bfloat16), "col", scatter_dimension=0, tiled=True
    )
    sigmoid_gate = jax.nn.sigmoid(first_pre)
    grad_pre = (
        grad_hidden.astype(jnp.float32) * sigmoid_gate * (1.0 + first_pre * (1.0 - sigmoid_gate))
    ).astype(jnp.bfloat16)
    first_term = (
        lax.dot_general(first_agg, grad_pre, contract_rows, preferred_element_type=jnp.float32)
        * norm_scale
    )
    grad_first = lax.psum(first_term, ("row", "col"))
    return (embedding, grad_first, grad_second)


def solution(mesh):
    placed = (
        P(("row", "col"), None),
        P("row", "col", None, None, None),
        P("row", "col", None),
        P("row", "col"),
        P("row", "col", None, None),
        P("row", "col"),
        P("col", None),
        P(),
        P(),
        P(("row", "col"), None),
    )
    return jax.shard_map(
        local,
        mesh=mesh,
        in_specs=placed,
        out_specs=(P(("row", "col"), None), P(), P()),
        check_vma=False,
    )
```

profile of v0, /device:TPU:2, one launch (start us, length us, event | category | flops | bytes accessed | tf_op | source)
XLA Modules:
  0.0 899.5 jit_solution(7173406365842705599)
XLA Ops:
  7.2 2.1 convolution_convert_fusion
  9.4 0.7 all-gather.5.cloned.1.call-update
  10.2 41.6 %all-gather.11.cloned.1.call-done = bf16[1024,512]{1,0:T(8,128)(2,1)} async-done(((bf16[128,512]{1,0:T(8,128)(2,1)}), bf16[1024,512]{1,0:T(8,128)(2,1)}) %all-gather.11.cloned.1.call-update) | async-done | bytes 1048592 | tf_op jit(solution)/shard_map/all_gather | solution.py:86
  51.8 38.6 %all-gather.5.cloned.1.call-done = bf16[1024,512]{1,0:T(8,128)(2,1)} async-done(((bf16[128,512]{1,0:T(8,128)(2,1)}), bf16[1024,512]{1,0:T(8,128)(2,1)}) %all-gather.5.cloned.1.call-update) | async-done | bytes 1048592 | tf_op jit(solution)/shard_map/all_gather | solution.py:56
  90.4 4.9 broadcast_select_fusion
  95.4 0.6 copy-done.14
  96.0 0.1 copy.17
  96.1 0.1 reshape.300
  96.2 0.1 copy.18
  96.3 0.1 reshape.308
  96.3 0.1 copy.19
  96.4 0.1 reshape.316
  96.5 0.1 copy.20
  96.6 0.1 reshape.324
  96.7 0.1 fusion.29
  96.8 0.1 fusion.30
  96.9 0.1 fusion.27
  97.0 118.1 %all-reduce.11.cloned.1.call-done = (bf16[8,128,512]{2,1,0:T(8,128)(2,1)}, bf16[8,128,512]{2,1,0:T(8,128)(2,1)}, bf16[8,128,512]{2,1,0:T(8,128)(2,1)}, bf16[8,128,512]{2,1,0:T(8,128)(2,1)}) async-done(((bf16[8,128,512]{2,1,0:T(8,128)(2,1)}, bf16[8,128,512]{2,1,0:T(8,128)(2,1)}, bf16[8,128,512]{2,1,0:T(8,128)(2,1)}, bf16[8,128,512]{2,1,0:T(8,128)(2,1)}), (bf16[8,128,512]{2,1,0:T(8,128)(2,1)}, ...) | async-done | bytes 4194320 | tf_op jit(solution)/shard_map/psum | solution.py:10
  215.1 3.2 gather_fusion
  218.3 3.4 gather_fusion.1
  221.8 3.6 fusion.5
  225.4 1.8 fusion.8
  227.2 3.3 gather_fusion.2
  230.5 3.5 fusion.11
  234.0 3.3 gather_fusion.3
  237.3 5.1 fusion.2
  242.4 39.5 %reduce-scatter.4.cloned.1.call-done = bf16[128,512]{1,0:T(8,128)(2,1)} async-done(((bf16[1024,512]{1,0:T(8,128)(2,1)}), bf16[128,512]{1,0:T(8,128)(2,1)}) %reduce-scatter.4.cloned.1.call-update) | async-done | bytes 131088 | tf_op jit(solution)/shard_map/reduce_scatter | solution.py:58
  281.9 1.8 multiply_convert_fusion.1
  283.8 0.5 all-gather.9.cloned.1.call-update
  284.4 36.8 %all-gather.7.cloned.1.call-done = bf16[1024,512]{1,0:T(8,128)(2,1)} async-done(((bf16[128,512]{1,0:T(8,128)(2,1)}), bf16[1024,512]{1,0:T(8,128)(2,1)}) %all-gather.7.cloned.1.call-update) | async-done | bytes 1048592 | tf_op jit(solution)/shard_map/all_gather | solution.py:63
  321.2 3.3 broadcast_select_fusion.10
  324.6 0.0 reduce-scatter.6.cloned.1.call-start
  324.6 0.6 copy-done.17
  325.2 50.8 %all-gather.9.cloned.1.call-done = bf16[4096,512]{1,0:T(8,128)(2,1)} async-done(((bf16[512,512]{1,0:T(8,128)(2,1)}), bf16[4096,512]{1,0:T(8,128)(2,1)}) %all-gather.9.cloned.1.call-update) | async-done | bytes 4194320 | tf_op jit(solution)/shard_map/all_gather | solution.py:67
  376.0 3.8 gather_fusion.8
  379.8 130.5 %all-reduce.9.cloned.1.call-done = (bf16[8,128,512]{2,1,0:T(8,128)(2,1)}, bf16[8,128,512]{2,1,0:T(8,128)(2,1)}, bf16[8,128,512]{2,1,0:T(8,128)(2,1)}, bf16[8,128...) async-done(((bf16[8,128,512]{2,1,0:T(8,128)(2,1)}, ...) | async-done | bytes 8388624 | tf_op jit(solution)/shard_map/psum | solution.py:10
  510.3 3.2 gather_fusion.4
  513.5 3.4 fusion.4
  517.0 3.3 gather_fusion.5
  520.2 3.4 fusion.7
  523.6 3.3 gather_fusion.6
  527.0 3.5 fusion.10
  530.4 3.3 gather_fusion.7
  533.7 2.2 fusion.12
  536.0 0.6 copy-done.8
  536.6 3.6 fusion.1
  540.3 3.3 gather_fusion.9
  543.6 3.2 gather_fusion.10
  546.8 3.3 gather_fusion.11
  550.1 3.3 gather_fusion.12
  553.4 2.2 fusion.3
  555.6 0.5 fusion.6
  556.1 1.1 copy-done.4
  557.2 0.5 fusion.9
  557.7 1.1 copy-done.6
  558.8 1.7 fusion
  560.6 19.0 %reduce-scatter.6.cloned.1.call-done = bf16[128,512]{1,0:T(8,128)(2,1)} async-done(((bf16[1024,512]{1,0:T(8,128)(2,1)}), bf16[128,512]{1,0:T(8,128)(2,1)}) %reduce-scatter.6.cloned.1.call-update) | async-done | bytes 131088 | tf_op jit(solution)/shard_map/reduce_scatter | solution.py:72
  579.5 2.2 convolution_multiply_fusion
  581.8 38.6 %reduce-scatter.8.cloned.1.call-done = bf16[128,512]{1,0:T(8,128)(2,1)} async-done(((bf16[1024,512]{1,0:T(8,128)(2,1)}), bf16[128,512]{1,0:T(8,128)(2,1)}) %reduce-scatter.8.cloned.1.call-update) | async-done | bytes 131088 | tf_op jit(solution)/shard_map/reduce_scatter | solution.py:88
  620.3 2.3 convolution_multiply_fusion.1
  622.6 0.9 convolution_convert_fusion.1
  623.5 265.8 %all-reduce.7.cloned.1.call-done = (f32[512,512]{1,0:T(8,128)}, f32[512,512]{1,0:T(8,128)}) async-done(((f32[512,512]{1,0:T(8,128)}, f32[512,512]{1,0:T(8,128)}), (f32[512,512]{1,0:T(8,128)}, f32[512,512]{1,0:T(8,128)})) %all-reduce.7.cloned.1.call-update) | async-done | bytes 2097168 | tf_op jit(solution)/shard_map/psum | solution.py:99
  889.3 2.4 copy.47
  891.7 1.0 copy.48
  (56 shorter events, 0.6 us)
Async XLA Ops:
  7.2 274.7 %copy-start = (bf16[512,512]{1,0:T(8,128)(2,1)S(1)}, bf16[512,512]{1,0:T(8,128)(2,1)}, u32[]{:S(2)}) copy-start(bf16[512,512]{1,0:T(8,128)(2,1)} %param.17) | copy-start | bytes 1572868
  7.2 44.6 %all-gather.11.cloned.1.call-start = ((), (), s32[]{:S(2)}) async-start(), calls=%async_computation.8 | async-start | bytes 1179648 | tf_op jit(solution)/shard_map/all_gather | solution.py:86
  9.4 81.0 %all-gather.5.cloned.1.call-start = ((), (), s32[]{:S(2)}) async-start(), calls=%async_computation.3 | async-start | bytes 1179648 | tf_op jit(solution)/shard_map/all_gather | solution.py:56
  10.1 205.0 %all-reduce.11.cloned.1.call-start = ((), (), s32[]{:S(2)}) async-start(), calls=%async_computation.12 | async-start | bytes 8388608 | tf_op jit(solution)/shard_map/psum | solution.py:10
  95.3 0.7 copy-start.14
  95.3 1.4 copy-start.15
  95.3 186.6 %reduce-scatter.4.cloned.1.call-start = ((), (), s32[]{:S(2)}) async-start(), calls=%async_computation.4 | async-start | bytes 1179648 | tf_op jit(solution)/shard_map/reduce_scatter | solution.py:58
  218.3 3.4 copy-start.2
  221.8 3.6 copy-start.5
  242.4 78.8 %all-gather.7.cloned.1.call-start = ((), (), s32[]{:S(2)}) async-start(), calls=%async_computation.5 | async-start | bytes 1179648 | tf_op jit(solution)/shard_map/all_gather | solution.py:63
  283.8 92.3 %all-gather.9.cloned.1.call-start = ((), (), s32[]{:S(2)}) async-start(), calls=%async_computation.6 | async-start | bytes 4718592 | tf_op jit(solution)/shard_map/all_gather | solution.py:67
  284.3 225.9 %all-reduce.9.cloned.1.call-start = ((), (), s32[]{:S(2)}) async-start(), calls=%async_computation.11 | async-start | bytes 16777216 | tf_op jit(solution)/shard_map/psum | solution.py:10
  324.5 0.7 copy-start.17
  324.6 255.0 %reduce-scatter.6.cloned.1.call-start = ((), (), s32[]{:S(2)}) async-start(), calls=%async_computation.7 | async-start | bytes 1179648 | tf_op jit(solution)/shard_map/reduce_scatter | solution.py:72
  533.7 2.2 copy-start.7
  533.7 2.9 copy-start.8
  533.7 2.9 copy-start.13
  540.2 80.1 %reduce-scatter.8.cloned.1.call-start = ((), (), s32[]{:S(2)}) async-start(), calls=%async_computation.9 | async-start | bytes 1179648 | tf_op jit(solution)/shard_map/reduce_scatter | solution.py:88
  553.4 2.2 copy-start.3
  555.6 1.6 copy-start.4
  557.2 1.6 copy-start.6
  558.8 20.7 %copy-start.11 = (bf16[128,512]{1,0:T(8,128)(2,1)S(1)}, bf16[128,512]{1,0:T(8,128)(2,1)}, u32[]{:S(2)}) copy-start(bf16[128,512]{1,0:T(8,128)(2,1)} %param.19) | copy-start | bytes 393220
  560.5 59.8 %copy-start.16 = (bf16[128,512]{1,0:T(8,128)(2,1)S(1)}, bf16[128,512]{1,0:T(8,128)(2,1)}, u32[]{:S(2)}) copy-start(bf16[128,512]{1,0:T(8,128)(2,1)} %reduce-scatter.4.cloned.1.call-done) | copy-start | bytes 393220
  560.5 328.8 %all-reduce.7.cloned.1.call-start = ((), (), s32[]{:S(2)}) async-start(), calls=%async_computation.10 | async-start | bytes 4194304 | tf_op jit(solution)/shard_map/psum | solution.py:99
  581.8 40.8 %copy-start.9 = (bf16[512,512]{1,0:T(8,128)(2,1)S(1)}, bf16[512,512]{1,0:T(8,128)(2,1)}, u32[]{:S(2)}) copy-start(bf16[512,512]{1,0:T(8,128)(2,1)} %param.18) | copy-start | bytes 1572868
  581.8 40.9 %copy-start.12 = (bf16[128,512]{1,0:T(8,128)(2,1)S(1)}, bf16[128,512]{1,0:T(8,128)(2,1)}, u32[]{:S(2)}) copy-start(bf16[128,512]{1,0:T(8,128)(2,1)} %reduce-scatter.6.cloned.1.call-done) | copy-start | bytes 393220
  889.3 2.4 copy-start.10
  889.3 3.4 copy-start.1
Sparse Core Ops, SparseCore 0:
  10.3 41.3 all-gather.10
  53.5 36.7 all-gather.4
  95.5 119.5 all-reduce.10
  242.5 39.3 reduce-scatter.3
  284.1 37.0 all-gather.6
  322.9 53.1 all-gather.8
  380.7 129.5 all-reduce.8
  540.4 39.1 reduce-scatter.5
  582.7 37.6 reduce-scatter.7
  626.3 262.9 all-reduce.6
where the time goes:
time: 901 us; the launch traced here: 900 us
  waiting for transfers between devices  781 us (87%)
  local copies, waits for them, and re-layouts  51.3 us (6%)
  matrix products  44.3 us (5%)
  between operations  14.3 us (2%)
    psum x1, waiting for transfers between devices, local(): grad_first = lax.psum(first_term, ('row', 'col'))  266 us
    psum x2, waiting for transfers between devices, spread(): return lax.psum(jnp.where(mine, shard, jnp.zeros_like(shard)), axis)  249 us
    all_gather x1, waiting for transfers between devices, local(): whole_cache = lax.all_gather(hist_cache, 'col', axis=0, tiled=True)  50.8 us
    all_gather x1, waiting for transfers between devices, local(): grad_panel = lax.all_gather(grad_agg, 'col', axis=0, tiled=True)  41.6 us
    gather x12, local copies, waits for them, and re-layouts, pick_tiles(): picked = blocks[tile_ids]  39.5 us
    reduce_scatter x1, waiting for transfers between devices, local(): lax.psum_scatter(first_sum.astype(jnp.bfloat16), 'col', scatter_dimension...  39.5 us
    all_gather x1, waiting for transfers between devices, local(): feat_panel = lax.all_gather(features, 'col', axis=0, tiled=True)  38.6 us
    reduce_scatter x1, waiting for transfers between devices, local(): lax.psum_scatter(back_sum.astype(jnp.bfloat16), 'col', scatter_dimension=...  38.6 us
  transfers between devices with their start and end apart: 10, of which 10 were waited for; matrix products, arithmetic and copies ran while one was open for 3% of the time, Pallas kernels for 0%

commit v1 on v0

--- a/solution.py
+++ b/solution.py
@@ -1,8 +1,38 @@
+import functools
 import math
 import jax
 import jax.numpy as jnp
 from jax import lax
 from jax.sharding import PartitionSpec as P
+
+
+def resolve_meshes(my_tile, axis_k):
+    k_now, wide_out, carry = (lax.axis_size("col"), lax.axis_index("col"), my_tile.shape[axis_k])
+    in_order = [b * k_now if i == axis_k else b for i, b in enumerate(my_tile.shape)]
+    block_now = lax.dynamic_update_slice_in_dim(
+        jnp.zeros(in_order, my_tile.dtype), my_tile, wide_out * carry, axis=axis_k
+    )
+    r_now = newest = my_tile
+    for to_i in range(1, k_now // 2 + 1):
+        r_now = lax.ppermute(
+            r_now, axis_name="col", perm=list(map(lambda i: (i, (i + 1) % k_now), range(k_now)))
+        )
+        block_now = lax.dynamic_update_slice_in_dim(
+            block_now, r_now, (wide_out - to_i) % k_now * carry, axis=axis_k
+        )
+        if 2 * to_i < k_now:
+            newest = lax.ppermute(
+                newest,
+                axis_name="col",
+                perm=list(map(lambda i: (i, (i - 1) % k_now), range(k_now))),
+            )
+            block_now = lax.dynamic_update_slice_in_dim(
+                block_now, newest, (wide_out + to_i) % k_now * carry, axis=axis_k
+            )
+    return block_now
+
+
+rest_bench_on_mesh = functools.partial(resolve_meshes, axis_k=0)
 
 
 def spread(shard, axis, root):
@@ -83,7 +113,7 @@
         * norm_scale
     )
     grad_second = lax.psum(second_term, ("row", "col"))
-    grad_panel = lax.all_gather(grad_agg, "col", axis=0, tiled=True)
+    grad_panel = rest_bench_on_mesh(grad_agg)
     back_sum = aggregate(grad_panel, tile_data, tile_ids, tile_counts)
     grad_hidden = lax.psum_scatter(
         back_sum.astype(jnp.bfloat16), "col", scatter_dimension=0, tiled=True

time: 901 us -> 861 us (0.956)
  waiting for transfers between devices: 781 us -> 730 us
  starting transfers between devices: 0.41 us -> 13.5 us
    all_gather x1 -> x0, waiting for transfers between devices: 41.6 us -> none  [local(): grad_panel = lax.all_gather(grad_agg, 'col', axis=0, tiled=True)]
    all_gather x1, waiting for transfers between devices: 38.6 us -> 12.3 us  [local(): feat_panel = lax.all_gather(features, 'col', axis=0, tiled=True)]
    ppermute x0 -> x7, waiting for transfers between devices: none -> 16.5 us  [the longest x4 14.4 us: resolve_meshes(): lax.ppermute(r_now, axis_name='col', perm=list(map(lambda i: (i, (i + 1)...]
    ppermute x0 -> x7, starting transfers between devices: none -> 13 us  [the longest x3 10.9 us: resolve_meshes(): lax.ppermute(newest, axis_name='col', perm=list(map(lambda i: (i, (i - 1)...]
  transfers between devices with their start and end apart: 10 -> 16, of which waited for: 10 -> 15; matrix products, arithmetic and copies ran while one was open for 3% -> 4% of each run, Pallas kernels for 0% -> 0%
where the time goes in v1:
time: 861 us; the launch traced here: 860 us
  waiting for transfers between devices  730 us (85%)
  local copies, waits for them, and re-layouts  51.3 us (6%)
  matrix products  43.5 us (5%)
  between operations  14 us (2%)
  starting transfers between devices  13.5 us (2%)
    psum x1, waiting for transfers between devices, local(): grad_first = lax.psum(first_term, ('row', 'col'))  266 us
    psum x2, waiting for transfers between devices, spread(): return lax.psum(jnp.where(mine, shard, jnp.zeros_like(shard)), axis)  249 us
    all_gather x1, waiting for transfers between devices, local(): whole_cache = lax.all_gather(hist_cache, 'col', axis=0, tiled=True)  50.8 us
    reduce_scatter x1, waiting for transfers between devices, local(): lax.psum_scatter(first_sum.astype(jnp.bfloat16), 'col', scatter_dimension...  39.5 us
    gather x12, local copies, waits for them, and re-layouts, pick_tiles(): picked = blocks[tile_ids]  39.4 us
    reduce_scatter x1, waiting for transfers between devices, local(): lax.psum_scatter(back_sum.astype(jnp.bfloat16), 'col', scatter_dimension=...  38.5 us
    all_gather x1, waiting for transfers between devices, local(): hidden_panel = lax.all_gather(hidden_share, 'col', axis=0, tiled=True)  36.8 us
    dot_general x12, matrix products, pick_tiles(): jnp.einsum('atij,atjf->aif', masked, picked, preferred_element_type=jnp.f...  31.4 us
  transfers between devices with their start and end apart: 16, of which 15 were waited for; matrix products, arithmetic and copies ran while one was open for 4% of the time, Pallas kernels for 0%

profile of v1, /device:TPU:2, one launch (start us, length us, event | category | flops | bytes accessed | tf_op | source)
XLA Modules:
  0.0 860.1 jit_solution(14592207221688713583)
XLA Ops:
  7.2 0.7 all-gather.4.cloned.1.call-update
  8.0 0.2 copy-done
  8.2 1.2 constant_dynamic-update-slice_fusion.7
  9.4 2.0 collective-permute-start
  11.4 4.0 collective-permute-start.1
  15.5 3.4 collective-permute-done
  18.9 3.2 collective-permute-start.3
  22.1 2.9 collective-permute-done.2
  25.0 0.9 collective-permute-done.3
  25.9 3.7 collective-permute-start.5
  29.6 1.9 collective-permute-done.4
  31.6 1.2 collective-permute-done.5
  32.8 6.2 collective-permute-done.6
  39.0 12.3 %all-gather.4.cloned.1.call-done = bf16[1024,512]{1,0:T(8,128)(2,1)} async-done(((bf16[128,512]{1,0:T(8,128)(2,1)}), bf16[1024,512]{1,0:T(8,128)(2,1)}) %all-gather.4.cloned.1.call-update) | async-done | bytes 1048592 | tf_op jit(solution)/shard_map/all_gather | solution.py:86
  51.3 4.6 broadcast_select_fusion
  56.0 0.6 copy-done.12
  56.6 0.1 copy.17
  57.6 118.6 %all-reduce.11.cloned.1.call-done = (bf16[8,128,512]{2,1,0:T(8,128)(2,1)}, bf16[8,128,512]{2,1,0:T(8,128)(2,1)}, bf16[8,128,512]{2,1,0:T(8,128)(2,1)}, bf16[8,128,512]{2,1,0:T(8,128)(2,1)}) async-done(((bf16[8,128,512]{2,1,0:T(8,128)(2,1)}, bf16[8,128,512]{2,1,0:T(8,128)(2,1)}, bf16[8,128,512]{2,1,0:T(8,128)(2,1)}, bf16[8,128,512]{2,1,0:T(8,128)(2,1)}), (bf16[8,128,512]{2,1,0:T(8,128)(2,1)}, ...) | async-done | bytes 4194320 | tf_op jit(solution)/shard_map/psum | solution.py:40
  176.2 3.2 gather_fusion
  179.4 3.4 gather_fusion.1
  182.9 3.6 fusion.5
  186.4 1.8 fusion.8
  188.3 3.3 gather_fusion.2
  191.6 3.4 fusion.11
  195.0 3.3 gather_fusion.3
  198.3 5.1 fusion.2
  203.5 39.5 %reduce-scatter.4.cloned.1.call-done = bf16[128,512]{1,0:T(8,128)(2,1)} async-done(((bf16[1024,512]{1,0:T(8,128)(2,1)}), bf16[128,512]{1,0:T(8,128)(2,1)}) %reduce-scatter.4.cloned.1.call-update) | async-done | bytes 131088 | tf_op jit(solution)/shard_map/reduce_scatter | solution.py:88
  243.0 1.8 multiply_convert_fusion.1
  244.9 0.5 all-gather.8.cloned.1.call-update
  245.5 36.8 %all-gather.6.cloned.1.call-done = bf16[1024,512]{1,0:T(8,128)(2,1)} async-done(((bf16[128,512]{1,0:T(8,128)(2,1)}), bf16[1024,512]{1,0:T(8,128)(2,1)}) %all-gather.6.cloned.1.call-update) | async-done | bytes 1048592 | tf_op jit(solution)/shard_map/all_gather | solution.py:93
  282.3 3.3 broadcast_select_fusion.10
  285.6 0.2 reduce-scatter.6.cloned.1.call-start
  285.9 0.4 copy-done.16
  286.3 50.8 %all-gather.8.cloned.1.call-done = bf16[4096,512]{1,0:T(8,128)(2,1)} async-done(((bf16[512,512]{1,0:T(8,128)(2,1)}), bf16[4096,512]{1,0:T(8,128)(2,1)}) %all-gather.8.cloned.1.call-update) | async-done | bytes 4194320 | tf_op jit(solution)/shard_map/all_gather | solution.py:97
  337.1 3.8 gather_fusion.8
  340.9 130.3 %all-reduce.9.cloned.1.call-done = (bf16[8,128,512]{2,1,0:T(8,128)(2,1)}, bf16[8,128,512]{2,1,0:T(8,128)(2,1)}, bf16[8,128,512]{2,1,0:T(8,128)(2,1)}, bf16[8,128...) async-done(((bf16[8,128,512]{2,1,0:T(8,128)(2,1)}, ...) | async-done | bytes 8388624 | tf_op jit(solution)/shard_map/psum | solution.py:40
  471.2 3.2 gather_fusion.4
  474.4 3.4 fusion.4
  477.9 3.3 gather_fusion.5
  481.1 3.4 fusion.7
  484.5 3.3 gather_fusion.6
  487.8 3.4 fusion.10
  491.3 3.3 gather_fusion.7
  494.6 2.2 fusion.12
  496.8 0.6 copy-done.7
  497.4 3.6 fusion.1
  501.2 3.3 gather_fusion.9
  504.4 3.2 gather_fusion.10
  507.6 3.3 gather_fusion.11
  510.9 3.3 gather_fusion.12
  514.2 2.2 fusion.3
  516.5 0.5 fusion.6
  517.0 1.1 copy-done.3
  518.0 0.5 fusion.9
  518.5 1.1 copy-done.5
  519.6 1.7 fusion
  521.4 19.0 %reduce-scatter.6.cloned.1.call-done = bf16[128,512]{1,0:T(8,128)(2,1)} async-done(((bf16[1024,512]{1,0:T(8,128)(2,1)}), bf16[128,512]{1,0:T(8,128)(2,1)}) %reduce-scatter.6.cloned.1.call-update) | async-done | bytes 131088 | tf_op jit(solution)/shard_map/reduce_scatter | solution.py:102
  540.4 2.2 convolution_multiply_fusion
  542.6 38.5 %reduce-scatter.8.cloned.1.call-done = bf16[128,512]{1,0:T(8,128)(2,1)} async-done(((bf16[1024,512]{1,0:T(8,128)(2,1)}), bf16[128,512]{1,0:T(8,128)(2,1)}) %reduce-scatter.8.cloned.1.call-update) | async-done | bytes 131088 | tf_op jit(solution)/shard_map/reduce_scatter | solution.py:118
  581.1 2.3 convolution_multiply_fusion.1
  583.4 0.9 convolution_convert_fusion.1
  584.3 265.9 %all-reduce.7.cloned.1.call-done = (f32[512,512]{1,0:T(8,128)}, f32[512,512]{1,0:T(8,128)}) async-done(((f32[512,512]{1,0:T(8,128)}, f32[512,512]{1,0:T(8,128)}), (f32[512,512]{1,0:T(8,128)}, f32[512,512]{1,0:T(8,128)})) %all-reduce.7.cloned.1.call-update) | async-done | bytes 2097168 | tf_op jit(solution)/shard_map/psum | solution.py:129
  850.2 2.4 copy.55
  852.6 1.0 copy.56
  (73 shorter events, 1.5 us)
Async XLA Ops:
  7.2 1.0 copy-start
  7.2 44.1 %all-gather.4.cloned.1.call-start = ((), (), s32[]{:S(2)}) async-start(), calls=%async_computation.3 | async-start | bytes 1179648 | tf_op jit(solution)/shard_map/all_gather | solution.py:86
  7.9 168.3 %all-reduce.11.cloned.1.call-start = ((), (), s32[]{:S(2)}) async-start(), calls=%async_computation.11 | async-start | bytes 8388608 | tf_op jit(solution)/shard_map/psum | solution.py:40
  9.4 9.4 %collective-permute-start = (bf16[128,512]{1,0:T(8,128)(2,1)S(1)}, bf16[128,512]{1,0:T(8,128)(2,1)S(1)}, u32[]{:S(2)}, u32[]{:S(2)}) collective-permute-start(bf16[128,512]{1,0:T(8,128)(2,1)S(1)} %get-tuple-element.40), channel_id=1, source_target_pairs={{0,1},{1,2},{2,3},{3,4},{4,5},{5,6},{6,7},{7,0},{8,9},{9,10},{10,1... | collective-permute-start | bytes 393224 | tf_op jit(solution)/shard_map/ppermute | solution.py:17
  11.4 7.4 collective-permute-start.1
  18.9 6.2 collective-permute-start.2
  18.9 7.1 collective-permute-start.3
  25.0 6.5 collective-permute-start.4
  25.9 6.9 collective-permute-start.5
  31.6 7.5 collective-permute-start.6
  55.9 0.7 copy-start.12
  55.9 1.4 copy-start.13
  55.9 187.1 %reduce-scatter.4.cloned.1.call-start = ((), (), s32[]{:S(2)}) async-start(), calls=%async_computation.4 | async-start | bytes 1179648 | tf_op jit(solution)/shard_map/reduce_scatter | solution.py:88
  179.4 3.4 copy-start.1
  182.9 3.6 copy-start.4
  198.3 44.7 %copy-start.14 = (bf16[512,512]{1,0:T(8,128)(2,1)S(1)}, bf16[512,512]{1,0:T(8,128)(2,1)}, u32[]{:S(2)}) copy-start(bf16[512,512]{1,0:T(8,128)(2,1)} %param.17) | copy-start | bytes 1572868
  203.5 78.8 %all-gather.6.cloned.1.call-start = ((), (), s32[]{:S(2)}) async-start(), calls=%async_computation.5 | async-start | bytes 1179648 | tf_op jit(solution)/shard_map/all_gather | solution.py:93
  244.9 92.2 %all-gather.8.cloned.1.call-start = ((), (), s32[]{:S(2)}) async-start(), calls=%async_computation.6 | async-start | bytes 4718592 | tf_op jit(solution)/shard_map/all_gather | solution.py:97
  245.5 225.7 %all-reduce.9.cloned.1.call-start = ((), (), s32[]{:S(2)}) async-start(), calls=%async_computation.10 | async-start | bytes 16777216 | tf_op jit(solution)/shard_map/psum | solution.py:40
  285.6 0.7 copy-start.16
  285.6 254.7 %reduce-scatter.6.cloned.1.call-start = ((), (), s32[]{:S(2)}) async-start(), calls=%async_computation.7 | async-start | bytes 1179648 | tf_op jit(solution)/shard_map/reduce_scatter | solution.py:102
  494.6 2.2 copy-start.6
  494.6 2.9 copy-start.7
  494.6 2.9 copy-start.11
  501.1 80.0 %reduce-scatter.8.cloned.1.call-start = ((), (), s32[]{:S(2)}) async-start(), calls=%async_computation.8 | async-start | bytes 1179648 | tf_op jit(solution)/shard_map/reduce_scatter | solution.py:118
  514.2 2.2 copy-start.2
  516.4 1.6 copy-start.3
  518.0 1.6 copy-start.5
  519.6 20.7 %copy-start.9 = (bf16[128,512]{1,0:T(8,128)(2,1)S(1)}, bf16[128,512]{1,0:T(8,128)(2,1)}, u32[]{:S(2)}) copy-start(bf16[128,512]{1,0:T(8,128)(2,1)} %param.19) | copy-start | bytes 393220
  521.3 59.8 %copy-start.15 = (bf16[128,512]{1,0:T(8,128)(2,1)S(1)}, bf16[128,512]{1,0:T(8,128)(2,1)}, u32[]{:S(2)}) copy-start(bf16[128,512]{1,0:T(8,128)(2,1)} %reduce-scatter.4.cloned.1.call-done) | copy-start | bytes 393220
  521.3 328.9 %all-reduce.7.cloned.1.call-start = ((), (), s32[]{:S(2)}) async-start(), calls=%async_computation.9 | async-start | bytes 4194304 | tf_op jit(solution)/shard_map/psum | solution.py:129
  542.6 40.8 %copy-start.10 = (bf16[128,512]{1,0:T(8,128)(2,1)S(1)}, bf16[128,512]{1,0:T(8,128)(2,1)}, u32[]{:S(2)}) copy-start(bf16[128,512]{1,0:T(8,128)(2,1)} %reduce-scatter.6.cloned.1.call-done) | copy-start | bytes 393220
  850.2 2.4 copy-start.8
Sparse Core Ops, SparseCore 0:
  9.8 41.4 all-gather.3
  56.1 120.0 all-reduce.10
  203.6 39.3 reduce-scatter.3
  245.2 37.0 all-gather.5
  283.9 53.1 all-gather.7
  341.7 129.5 all-reduce.8
  501.2 39.1 reduce-scatter.5
  543.5 37.6 reduce-scatter.7
  587.3 262.9 all-reduce.6
